TPU v7x, 256 devices: a whole 4x4x8 slice. The times are simulated.
256 devices in a mesh: tiles: 16 (over y, z_lo, core), coef: 16 (over x, z_hi).
Axes of the slice: x: 4, y: 4, z: 8 (z_hi: 4, z_lo: 2; z = z_hi * 2 + z_lo), core: 2. Of those that a mesh axis runs over, the one named last changes fastest.
Arguments:
- fields: bfloat16 [256, 8192], P('coef', 'tiles'), may hold values from -6 to 6
- adjoints: bfloat16 [256, 8192], P('coef', 'tiles'), may hold values from -6 to 6
- couple: bfloat16 [30, 256, 256], replicated, may hold values from -0.0625 to 0.0625
- tmatrices: bfloat16 [64, 256, 256], P('tiles', 'coef'), may hold values from -0.375 to 0.375
- neighbours: int32 [8192, 30], P('tiles'), may hold values from -1 to 8191, as said below
- classes: int32 [8192], P('tiles'), may hold values from 0 to 63
Outputs:
- forward_out: bfloat16 [256, 8192], P('coef', 'tiles')
- adjoint_out: bfloat16 [256, 8192], P('coef', 'tiles')
Inputs may be any that keep to these rules, and one draw needn't show every extreme that they name: neighbours[i, m] is -1 or i + m - 15 for m < 15, or i + m - 14 for m >= 15; links are mutual: neighbours[i, m] = j >= 0 exactly when neighbours[j, 29 - m] = i; slots 15 - 1 and 15 are filled wherever the neighbouring pillar exists.
All inputs are finite; a program needn't handle non-finite values.
Results may differ from a plain program's by a relative error of at most 0.0037.
Values may be sent and summed in bfloat16 or wider, within the bound.
A program may use at most 64 MiB of HBM per device.

v0:
```python
import jax
import jax.numpy as jnp
from jax import lax
from jax.sharding import PartitionSpec as P

SLOTS = 30
HW = 15


def padded_2(cells, sides, width):
    for axis, dim in sides:
        count = lax.axis_size(axis)
        ends = count - 1
        head = lax.slice_in_dim(cells, 0, width, axis=dim)
        tail = lax.slice_in_dim(cells, cells.shape[dim] - width, cells.shape[dim], axis=dim)
        cells = jnp.concatenate(
            [
                lax.ppermute(tail, axis, [(i, (i + 1) % count) for i in range(ends)]),
                cells,
                lax.ppermute(head, axis, [((i + 1) % count, i) for i in range(ends)]),
            ],
            axis=dim,
        )
    return cells


def slot_columns(padded, weight_table, starts, width):
    pieces = [
        padded[:, start : start + width] * weight_table[slot][None, :]
        for slot, start in enumerate(starts)
    ]
    return jnp.stack(pieces, axis=1)


def local(fields, adjoints, couple, tmatrices, neighbours, classes):
    row_count = fields.shape[0]
    tile_len = fields.shape[1]
    coef_index = lax.axis_index("coef")
    is_valid = neighbours >= 0
    slot_weight = is_valid.astype(jnp.bfloat16).T
    forward_starts = [slot + (1 if slot >= HW else 0) for slot in range(SLOTS)]
    adjoint_starts = forward_starts[::-1]
    own_first = coef_index * row_count

    def translate(source, weight_table, starts, adjoint_mode):
        padded = padded_2(source, (("tiles", 1),), HW)
        own_mats = lax.dynamic_slice_in_dim(couple, own_first, row_count, 2 if adjoint_mode else 1)

        def add_piece(arrived):
            selected = slot_columns(arrived, weight_table, starts, tile_len)
            if adjoint_mode:
                block_mat = own_mats
                return jnp.einsum(
                    "nkr,kni->ri", block_mat, selected, preferred_element_type=jnp.float32
                )
            block_mat = own_mats
            return jnp.einsum(
                "nrk,kni->ri", block_mat, selected, preferred_element_type=jnp.float32
            )

        return add_piece(lax.all_gather(padded, "coef", axis=0, tiled=True))

    coupled = translate(fields, slot_weight, forward_starts, False).astype(jnp.bfloat16)
    class_rows = lax.all_gather(tmatrices, "tiles", axis=0, tiled=True)
    sub_table = class_rows
    picked = jnp.take(sub_table, classes, axis=0)
    applied = jnp.einsum(
        "irk,ki->ri",
        picked,
        lax.all_gather(coupled, "coef", axis=0, tiled=True),
        preferred_element_type=jnp.float32,
    )
    forward_out = (fields.astype(jnp.float32) - applied).astype(jnp.bfloat16)
    class_cols = lax.all_to_all(class_rows, "coef", split_axis=2, concat_axis=1, tiled=True)
    sub_table = class_cols
    picked = jnp.take(sub_table, classes, axis=0)
    scattered_sum = jnp.einsum(
        "irk,ri->ki",
        picked,
        lax.all_gather(adjoints, "coef", axis=0, tiled=True),
        preferred_element_type=jnp.float32,
    )
    scattered = scattered_sum.astype(jnp.bfloat16)
    returned = translate(scattered, slot_weight[::-1], adjoint_starts, True)
    adjoint_out = (adjoints.astype(jnp.float32) - returned).astype(jnp.bfloat16)
    return (forward_out, adjoint_out)


def solution(mesh):
    placed = (
        P("coef", "tiles"),
        P("coef", "tiles"),
        P(),
        P("tiles", "coef", None),
        P("tiles", None),
        P("tiles"),
    )
    return jax.shard_map(
        local,
        mesh=mesh,
        in_specs=placed,
        out_specs=(P("coef", "tiles"), P("coef", "tiles")),
        check_vma=False,
    )
```

profile of v0, /device:TPU:32, one launch (start us, length us, event | category | flops | bytes accessed | tf_op | source)
XLA Modules:
  0.0 260.7 jit_solution(10606946548636086392)
XLA Ops:
  0.6 0.8 fusion.138
  1.5 1.9 collective-permute-start
  3.4 3.6 %collective-permute-start.1 = (bf16[16,15]{1,0:T(8,128)(2,1)S(1)}, bf16[16,15]{1,0:T(8,128)(2,1)S(1)}, u32[]{:S(2)}, u32[]{:S(2)}) collective-permute-start(bf16[16,15]{1,0:T(8,128)(2,1)S(1)} %get-tuple-element.37), channel_id=1, source_target_pairs={{16,0},{32,16},{48,32},{64,48},{80,64},{96,80},{112,96},{128,112},... | collective-permute-start | bytes 1448 | tf_op jit(solution)/shard_map/ppermute | solution.py:20
  7.0 19.3 %all_gather.17 = bf16[64,16,256]{2,1,0:T(8,128)(2,1)S(1)} all-gather(bf16[4,16,256]{2,1,0:T(8,128)(2,1)} %param.9), channel_id=1, replica_groups=mesh['tiles'=16,'coef'=16] {'tiles'}, dimensions={0}, use_global_device_ids=true | all-gather | bytes 557056 | tf_op jit(solution)/shard_map/all_gather | solution.py:64
  26.3 1.3 copy.22
  27.6 1.5 reshape.63
  29.1 11.2 %all-to-all-start = ((bf16[16,2,8192]{2,1,0:T(2,128)(2,1)}), bf16[16,2,8192]{2,1,0:T(2,128)(2,1)S(1)}, u32[]{:S(2)}, u32[]{:S(2)}) async-start(bf16[16,2,8192]{2,1,0:T(2,128)(2,1)} %reshape.63), calls=%async_computation | async-start | bytes 1048576 | tf_op jit(solution)/shard_map/all_to_all | solution.py:74
  40.3 0.8 fusion.133
  41.4 0.7 compare_select_fusion
  42.1 0.7 compare_and_fusion
  42.8 50.0 %all_gather.18 = bf16[256,512]{1,0:T(8,128)(2,1)S(1)} all-gather(bf16[16,512]{1,0:T(8,128)(2,1)} %param.7), channel_id=1, replica_groups=mesh['tiles'=16,'coef'=16] {'coef'}, dimensions={0}, use_global_device_ids=true | all-gather | bytes 278528 | tf_op jit(solution)/shard_map/all_gather | solution.py:80
  92.8 3.4 %gather_fusion = bf16[512,16,256]{2,1,0:T(8,128)(2,1)} fusion(bf16[64,16,256]{2,1,0:T(8,128)(2,1)S(1)} %all_gather.17, s32[1024]{0:T(1024)S(1)} %pad_clamp_fusion), kind=kCustom, calls=%fused_computation | custom fusion | bytes 8390656 | tf_op jit(solution)/shard_map/jit(_take)/gather | solution.py:66
  96.2 0.2 copy.40
  96.5 42.1 %all_gather.15 = bf16[256,542]{1,0:T(8,128)(2,1)S(1)} all-gather(bf16[16,542]{1,0:T(8,128)(2,1)S(1)} %pad_maximum_fusion), channel_id=1, replica_groups=mesh['tiles'=16,'coef'=16] {'coef'}, dimensions={0}, use_global_device_ids=true | all-gather | bytes 294848 | tf_op jit(solution)/shard_map/all_gather | solution.py:61
  138.7 0.1 fusion.129
  138.9 0.1 fusion.127
  139.2 0.1 fusion.123
  139.5 0.1 fusion.119
  143.0 2.1 fusion.8
  145.1 40.5 %all_gather.16 = bf16[256,512]{1,0:T(8,128)(2,1)S(1)} all-gather(bf16[16,512]{1,0:T(8,128)(2,1)S(1)} %fusion.8), channel_id=1, replica_groups=mesh['tiles'=16,'coef'=16] {'coef'}, dimensions={0}, use_global_device_ids=true | all-gather | bytes 278528 | tf_op jit(solution)/shard_map/all_gather | solution.py:70
  185.6 0.2 copy.39
  185.9 0.7 reshape.64
  186.5 0.3 copy.24
  186.8 1.3 copy.25
  188.1 3.5 %gather_fusion.1 = bf16[512,256,16]{1,2,0:T(8,128)(2,1)} fusion(bf16[64,256,16]{1,2,0:T(8,128)(2,1)S(1)} %copy.25, s32[1024]{0:T(1024)S(1)} %pad_clamp_fusion), kind=kCustom, calls=%fused_computation.1 | custom fusion | bytes 8390656 | tf_op jit(solution)/shard_map/jit(_take)/gather | solution.py:76
  191.6 13.6 %multiply_reduce_fusion = (bf16[512,16]{1,0:T(8,128)(2,1)S(1)}, f32[512,16]{1,0:T(8,128)S(1)}) fusion(f32[512,256]{1,0:T(8,128)S(1)} %copy.40, bf16[512,256,16]{1,2,0:T(8,128)(2,1)} %gather_fusion.1, pred[512]{0:T(512)(128)(4,1)S(1)} %compare_and_fusion, bf16[512,16,256]{2,1,0:T(8,128)(2,1)} %gather_fusion, f32[512,256]{1,0:T(8,128)S(1)} %copy.39), kind=kLoop, calls=%fused_computation.2 | loop fusion | flops 16760832 | bytes 9486848
  205.4 1.9 collective-permute-start.2
  207.3 3.6 %collective-permute-start.3 = (bf16[16,15]{1,0:T(8,128)(2,1)S(1)}, bf16[16,15]{1,0:T(8,128)(2,1)S(1)}, u32[]{:S(2)}, u32[]{:S(2)}) collective-permute-start(bf16[16,15]{1,0:T(8,128)(2,1)S(1)} %get-tuple-element.35), channel_id=1, source_target_pairs={{16,0},{32,16},{48,32},{64,48},{80,64},{96,80},{112,96},{128,112},... | collective-permute-start | bytes 1448 | tf_op jit(solution)/shard_map/ppermute | solution.py:20
  211.0 0.6 fusion.134
  211.7 0.6 collective-permute-done.3
  212.3 41.8 %all_gather.19 = bf16[256,542]{1,0:T(8,128)(2,1)S(1)} all-gather(bf16[16,542]{1,0:T(8,128)(2,1)S(1)} %pad_maximum_fusion.1), channel_id=1, replica_groups=mesh['tiles'=16,'coef'=16] {'coef'}, dimensions={0}, use_global_device_ids=true | all-gather | bytes 294848 | tf_op jit(solution)/shard_map/all_gather | solution.py:61
  258.5 2.2 fusion.9
  (76 shorter events, 8.4 us)
Async XLA Ops:
  0.6 95.8 %copy-start.1 = (bf16[16,512]{1,0:T(8,128)(2,1)S(1)}, bf16[16,512]{1,0:T(8,128)(2,1)}, u32[]{:S(2)}) copy-start(bf16[16,512]{1,0:T(8,128)(2,1)} %param.6) | copy-start | bytes 49156
  1.5 95.0 %collective-permute-start = (bf16[16,15]{1,0:T(8,128)(2,1)S(1)}, bf16[16,15]{1,0:T(8,128)(2,1)S(1)}, u32[]{:S(2)}, u32[]{:S(2)}) collective-permute-start(bf16[16,15]{1,0:T(8,128)(2,1)S(1)} %get-tuple-element.36), channel_id=1, source_target_pairs={{0,16},{16,32},{32,48},{48,64},{64,80},{80,96},{96,112},{112,128},... | collective-permute-start | bytes 1448 | tf_op jit(solution)/shard_map/ppermute | solution.py:18
  3.4 93.1 %collective-permute-start.1 = (bf16[16,15]{1,0:T(8,128)(2,1)S(1)}, bf16[16,15]{1,0:T(8,128)(2,1)S(1)}, u32[]{:S(2)}, u32[]{:S(2)}) collective-permute-start(bf16[16,15]{1,0:T(8,128)(2,1)S(1)} %get-tuple-element.37), channel_id=1, source_target_pairs={{16,0},{32,16},{48,32},{64,48},{80,64},{96,80},{112,96},{128,112},... | collective-permute-start | bytes 1448 | tf_op jit(solution)/shard_map/ppermute | solution.py:20
  29.1 156.7 %all-to-all-start = ((bf16[16,2,8192]{2,1,0:T(2,128)(2,1)}), bf16[16,2,8192]{2,1,0:T(2,128)(2,1)S(1)}, u32[]{:S(2)}, u32[]{:S(2)}) async-start(bf16[16,2,8192]{2,1,0:T(2,128)(2,1)} %reshape.63), calls=%async_computation | async-start | bytes 1048576 | tf_op jit(solution)/shard_map/all_to_all | solution.py:74
  205.4 6.3 %collective-permute-start.2 = (bf16[16,15]{1,0:T(8,128)(2,1)S(1)}, bf16[16,15]{1,0:T(8,128)(2,1)S(1)}, u32[]{:S(2)}, u32[]{:S(2)}) collective-permute-start(bf16[16,15]{1,0:T(8,128)(2,1)S(1)} %get-tuple-element.34), channel_id=1, source_target_pairs={{0,16},{16,32},{32,48},{48,64},{64,80},{80,96},{96,112},{112,128},... | collective-permute-start | bytes 1448 | tf_op jit(solution)/shard_map/ppermute | solution.py:18
  207.3 5.0 %collective-permute-start.3 = (bf16[16,15]{1,0:T(8,128)(2,1)S(1)}, bf16[16,15]{1,0:T(8,128)(2,1)S(1)}, u32[]{:S(2)}, u32[]{:S(2)}) collective-permute-start(bf16[16,15]{1,0:T(8,128)(2,1)S(1)} %get-tuple-element.35), channel_id=1, source_target_pairs={{16,0},{32,16},{48,32},{64,48},{80,64},{96,80},{112,96},{128,112},... | collective-permute-start | bytes 1448 | tf_op jit(solution)/shard_map/ppermute | solution.py:20
  254.2 4.3 %copy-start = (bf16[30,256,256]{2,1,0:T(8,128)(2,1)S(1)}, bf16[30,256,256]{2,1,0:T(8,128)(2,1)}, u32[]{:S(2)}) copy-start(bf16[30,256,256]{2,1,0:T(8,128)(2,1)} %param.8) | copy-start | bytes 11796484
  254.2 4.3 %copy-start.2 = (bf16[16,512]{1,0:T(8,128)(2,1)S(1)}, bf16[16,512]{1,0:T(8,128)(2,1)}, u32[]{:S(2)}) copy-start(bf16[16,512]{1,0:T(8,128)(2,1)} %param.7) | copy-start | bytes 49156
where the time goes:
time: 261 us
  blocking collectives  194 us (74%)
  other arithmetic  24.9 us (10%)
  starting transfers between devices  22.3 us (9%)
  local copies, waits for them, and re-layouts  13.7 us (5%)
  matrix products  4.25 us (2%)
    all_gather x2, blocking collectives, translate(): return add_piece(lax.all_gather(padded, 'coef', axis=0, tiled=True))  84 us
    all_gather x1, blocking collectives, local(): lax.all_gather(adjoints, 'coef', axis=0, tiled=True)  50 us
    all_gather x1, blocking collectives, local(): lax.all_gather(coupled, 'coef', axis=0, tiled=True)  40.5 us
    unnamed x61, other arithmetic  21.7 us
    all_gather x1, blocking collectives, local(): class_rows = lax.all_gather(tmatrices, 'tiles', axis=0, tiled=True)  19.3 us
    all_to_all x1, starting transfers between devices, local(): lax.all_to_all(class_rows, 'coef', split_axis=2, concat_axis=1, tiled=True)  11.2 us
    ppermute x2, starting transfers between devices, padded_2(): lax.ppermute(head, axis, [((i + 1) % count, i) for i in range(ends)])  7.28 us
    gather x2, local copies, waits for them, and re-layouts, local(): picked = jnp.take(sub_table, classes, axis=0)  6.91 us
  transfers between devices with their start and end apart: 5, of which 1 were waited for; matrix products, arithmetic and copies ran while one was open for 6% of the time, Pallas kernels for 0%

commit v1 on v0

--- a/solution.py
+++ b/solution.py
@@ -58,7 +58,11 @@
                 "nrk,kni->ri", block_mat, selected, preferred_element_type=jnp.float32
             )
 
-        return add_piece(lax.all_gather(padded, "coef", axis=0, tiled=True))
+        return add_piece(
+            jnp.concatenate(
+                lax.all_to_all(jnp.stack([padded] * lax.axis_size("coef")), "coef", 0, 0), axis=0
+            )
+        )
 
     coupled = translate(fields, slot_weight, forward_starts, False).astype(jnp.bfloat16)
     class_rows = lax.all_gather(tmatrices, "tiles", axis=0, tiled=True)

time: 261 us -> 205 us (0.79)
  blocking collectives: 194 us -> 113 us
  waiting for transfers between devices: 0.59 us -> 22.4 us
    all_gather x2 -> x0, blocking collectives: 84 us -> none  [translate(): return add_piece(lax.all_gather(padded, 'coef', axis=0, tiled=True))]
    all_to_all x0 -> x2, waiting for transfers between devices: none -> 21.1 us  [translate(): lax.all_to_all(jnp.stack([padded] * lax.axis_size('coef')), 'coef', 0, 0)]
    all_to_all x1, starting transfers between devices: 11.2 us -> 3.57 us  [local(): lax.all_to_all(class_rows, 'coef', split_axis=2, concat_axis=1, tiled=True)]
    all_to_all x0 -> x2, starting transfers between devices: none -> 7.08 us  [translate(): lax.all_to_all(jnp.stack([padded] * lax.axis_size('coef')), 'coef', 0, 0)]
    all_gather x1, blocking collectives: 40.5 us -> 45.6 us  [local(): lax.all_gather(coupled, 'coef', axis=0, tiled=True)]
  transfers between devices with their start and end apart: 5 -> 7, of which waited for: 1 -> 3; matrix products, arithmetic and copies ran while one was open for 6% -> 8% of each run, Pallas kernels for 0% -> 0%
where the time goes in v1:
time: 205 us; the launch traced here: 203 us
  blocking collectives  113 us (55%)
  other arithmetic  24.9 us (12%)
  waiting for transfers between devices  22.4 us (11%)
  starting transfers between devices  21.8 us (11%)
  local copies, waits for them, and re-layouts  15.1 us (7%)
  matrix products  4.25 us (2%)
    all_gather x1, blocking collectives, local(): lax.all_gather(adjoints, 'coef', axis=0, tiled=True)  48.3 us
    all_gather x1, blocking collectives, local(): lax.all_gather(coupled, 'coef', axis=0, tiled=True)  45.6 us
    unnamed x61, other arithmetic  21.7 us
    all_to_all x2, waiting for transfers between devices, translate(): lax.all_to_all(jnp.stack([padded] * lax.axis_size('coef')), 'coef', 0, 0)  21.1 us
    all_gather x1, blocking collectives, local(): class_rows = lax.all_gather(tmatrices, 'tiles', axis=0, tiled=True)  19.2 us
    ppermute x2, starting transfers between devices, padded_2(): lax.ppermute(head, axis, [((i + 1) % count, i) for i in range(ends)])  7.28 us
    all_to_all x2, starting transfers between devices, translate(): lax.all_to_all(jnp.stack([padded] * lax.axis_size('coef')), 'coef', 0, 0)  7.08 us
    gather x2, local copies, waits for them, and re-layouts, local(): picked = jnp.take(sub_table, classes, axis=0)  6.91 us
  transfers between devices with their start and end apart: 7, of which 3 were waited for; matrix products, arithmetic and copies ran while one was open for 8% of the time, Pallas kernels for 0%

profile of v1, /device:TPU:32, one launch (start us, length us, event | category | flops | bytes accessed | tf_op | source)
XLA Modules:
  0.0 202.9 jit_solution(68533548662876610)
XLA Ops:
  0.6 0.8 fusion.138
  1.4 1.9 collective-permute-start
  3.3 3.6 %collective-permute-start.1 = (bf16[16,15]{1,0:T(8,128)(2,1)S(1)}, bf16[16,15]{1,0:T(8,128)(2,1)S(1)}, u32[]{:S(2)}, u32[]{:S(2)}) collective-permute-start(bf16[16,15]{1,0:T(8,128)(2,1)S(1)} %get-tuple-element.37), channel_id=1, source_target_pairs={{16,0},{32,16},{48,32},{64,48},{80,64},{96,80},{112,96},{128,112},... | collective-permute-start | bytes 1448 | tf_op jit(solution)/shard_map/ppermute | solution.py:20
  7.0 0.8 fusion.133
  7.8 19.2 %all_gather.10 = bf16[64,16,256]{2,1,0:T(8,128)(2,1)S(1)} all-gather(bf16[4,16,256]{2,1,0:T(8,128)(2,1)} %param.9), channel_id=1, replica_groups=mesh['tiles'=16,'coef'=16] {'tiles'}, dimensions={0}, use_global_device_ids=true | all-gather | bytes 557056 | tf_op jit(solution)/shard_map/all_gather | solution.py:68
  27.1 48.3 %all_gather.11 = bf16[256,512]{1,0:T(8,128)(2,1)S(1)} all-gather(bf16[16,512]{1,0:T(8,128)(2,1)} %param.7), channel_id=1, replica_groups=mesh['tiles'=16,'coef'=16] {'coef'}, dimensions={0}, use_global_device_ids=true | all-gather | bytes 278528 | tf_op jit(solution)/shard_map/all_gather | solution.py:84
  75.5 0.7 compare_select_fusion
  76.2 0.8 pad_maximum_fusion
  77.0 0.8 stack.224
  77.7 3.5 %all-to-all-start = ((bf16[16,16,542]{2,1,0:T(8,128)(2,1)}), bf16[16,16,542]{2,1,0:T(8,128)(2,1)S(1)}, u32[]{:S(2)}, u32[]{:S(2)}) async-start(bf16[16,16,542]{2,1,0:T(8,128)(2,1)} %stack.224), calls=%async_computation | async-start | bytes 655360 | tf_op jit(solution)/shard_map/all_to_all | solution.py:63
  81.3 1.3 copy.22
  82.6 1.5 reshape.75
  84.1 3.4 %gather_fusion = bf16[512,16,256]{2,1,0:T(8,128)(2,1)} fusion(bf16[64,16,256]{2,1,0:T(8,128)(2,1)S(1)} %all_gather.10, s32[1024]{0:T(1024)S(1)} %pad_clamp_fusion), kind=kCustom, calls=%fused_computation | custom fusion | bytes 8390656 | tf_op jit(solution)/shard_map/jit(_take)/gather | solution.py:70
  87.5 0.2 copy.40
  88.0 6.5 %all-to-all-done = bf16[16,16,542]{2,1,0:T(8,128)(2,1)S(1)} async-done(((bf16[16,16,542]{2,1,0:T(8,128)(2,1)}), bf16[16,16,542]{2,1,0:T(8,128)(2,1)S(1)}, u32[]{:S(2)}, u32[]{:S(2)}) %all-to-all-start) | async-done | bytes 277536 | tf_op jit(solution)/shard_map/all_to_all | solution.py:63
  94.5 3.6 %all-to-all-start.1 = ((bf16[16,2,8192]{2,1,0:T(2,128)(2,1)}), bf16[16,2,8192]{2,1,0:T(2,128)(2,1)S(1)}, u32[]{:S(2)}, u32[]{:S(2)}) async-start(bf16[16,2,8192]{2,1,0:T(2,128)(2,1)} %reshape.75), calls=%async_computation.1 | async-start | bytes 1048576 | tf_op jit(solution)/shard_map/all_to_all | solution.py:78
  102.4 2.1 %fusion.8 = bf16[16,512]{1,0:T(8,128)(2,1)S(1)} fusion(bf16[256,30,512]{2,0,1:T(8,128)(2,1)S(1)} %fusion.73, bf16[30,256,256]{2,1,0:T(8,128)(2,1)} %param.8, s32[]{:T(128)S(6)} %select_n.19), kind=kOutput, calls=%fused_computation.9 | convolution fusion | flops 125837312 | bytes 8126468 | tf_op jit(solution)/shard_map/nrk,kni->ri/dot_general | solution.py:57
  104.4 45.6 %all_gather.9 = bf16[256,512]{1,0:T(8,128)(2,1)S(1)} all-gather(bf16[16,512]{1,0:T(8,128)(2,1)S(1)} %fusion.8), channel_id=1, replica_groups=mesh['tiles'=16,'coef'=16] {'coef'}, dimensions={0}, use_global_device_ids=true | all-gather | bytes 278528 | tf_op jit(solution)/shard_map/all_gather | solution.py:74
  150.1 0.2 copy.39
  150.3 0.7 reshape.76
  151.0 0.3 copy.24
  151.3 1.3 copy.25
  152.6 3.5 %gather_fusion.1 = bf16[512,256,16]{1,2,0:T(8,128)(2,1)} fusion(bf16[64,256,16]{1,2,0:T(8,128)(2,1)S(1)} %copy.25, s32[1024]{0:T(1024)S(1)} %pad_clamp_fusion), kind=kCustom, calls=%fused_computation.1 | custom fusion | bytes 8390656 | tf_op jit(solution)/shard_map/jit(_take)/gather | solution.py:80
  156.1 13.6 %multiply_reduce_fusion = (bf16[512,16]{1,0:T(8,128)(2,1)S(1)}, f32[512,16]{1,0:T(8,128)S(1)}) fusion(f32[512,256]{1,0:T(8,128)S(1)} %copy.40, bf16[512,256,16]{1,2,0:T(8,128)(2,1)} %gather_fusion.1, pred[512]{0:T(512)(128)(4,1)S(1)} %compare_and_fusion, bf16[512,16,256]{2,1,0:T(8,128)(2,1)} %gather_fusion, f32[512,256]{1,0:T(8,128)S(1)} %copy.39), kind=kLoop, calls=%fused_computation.2 | loop fusion | flops 16760832 | bytes 9486848
  169.9 1.9 collective-permute-start.2
  171.8 3.6 %collective-permute-start.3 = (bf16[16,15]{1,0:T(8,128)(2,1)S(1)}, bf16[16,15]{1,0:T(8,128)(2,1)S(1)}, u32[]{:S(2)}, u32[]{:S(2)}) collective-permute-start(bf16[16,15]{1,0:T(8,128)(2,1)S(1)} %get-tuple-element.35), channel_id=1, source_target_pairs={{16,0},{32,16},{48,32},{64,48},{80,64},{96,80},{112,96},{128,112},... | collective-permute-start | bytes 1448 | tf_op jit(solution)/shard_map/ppermute | solution.py:20
  175.4 1.3 collective-permute-done.3
  176.8 0.7 stack.256
  177.6 3.5 %all-to-all-start.2 = ((bf16[16,16,542]{2,1,0:T(8,128)(2,1)}), bf16[16,16,542]{2,1,0:T(8,128)(2,1)S(1)}, u32[]{:S(2)}, u32[]{:S(2)}) async-start(bf16[16,16,542]{2,1,0:T(8,128)(2,1)} %stack.256), calls=%async_computation.2 | async-start | bytes 655360 | tf_op jit(solution)/shard_map/all_to_all | solution.py:63
  181.2 0.6 fusion.134
  181.8 14.6 %all-to-all-done.2 = bf16[16,16,542]{2,1,0:T(8,128)(2,1)S(1)} async-done(((bf16[16,16,542]{2,1,0:T(8,128)(2,1)}), bf16[16,16,542]{2,1,0:T(8,128)(2,1)S(1)}, u32[]{:S(2)}, u32[]{:S(2)}) %all-to-all-start.2) | async-done | bytes 277536 | tf_op jit(solution)/shard_map/all_to_all | solution.py:63
  200.8 2.2 %fusion.9 = bf16[16,512]{1,0:T(8,128)(2,1)} fusion(bf16[256,30,512]{2,0,1:T(8,128)(2,1)S(1)} %fusion.13, bf16[30,256,256]{2,1,0:T(8,128)(2,1)S(1)} %copy-done, s32[]{:T(128)S(6)} %select_n.19, bf16[16,512]{1,0:T(8,128)(2,1)S(1)} %copy-done.2), kind=kOutput, calls=%fused_computation.10 | convolution fusion | flops 125853696 | bytes 9863172 | tf_op jit(solution)/shard_map/nkr,kni->ri/dot_general | solution.py:53
  (82 shorter events, 8.9 us)
Async XLA Ops:
  0.6 87.3 %copy-start.3 = (s32[512]{0:T(512)S(1)}, s32[512]{0:T(512)}, u32[]{:S(2)}) copy-start(s32[512]{0:T(512)} %param.11) | copy-start | bytes 6148
  1.4 74.8 %collective-permute-start = (bf16[16,15]{1,0:T(8,128)(2,1)S(1)}, bf16[16,15]{1,0:T(8,128)(2,1)S(1)}, u32[]{:S(2)}, u32[]{:S(2)}) collective-permute-start(bf16[16,15]{1,0:T(8,128)(2,1)S(1)} %get-tuple-element.36), channel_id=1, source_target_pairs={{0,16},{16,32},{32,48},{48,64},{64,80},{80,96},{96,112},{112,128},... | collective-permute-start | bytes 1448 | tf_op jit(solution)/shard_map/ppermute | solution.py:18
  3.3 72.8 %collective-permute-start.1 = (bf16[16,15]{1,0:T(8,128)(2,1)S(1)}, bf16[16,15]{1,0:T(8,128)(2,1)S(1)}, u32[]{:S(2)}, u32[]{:S(2)}) collective-permute-start(bf16[16,15]{1,0:T(8,128)(2,1)S(1)} %get-tuple-element.37), channel_id=1, source_target_pairs={{16,0},{32,16},{48,32},{64,48},{80,64},{96,80},{112,96},{128,112},... | collective-permute-start | bytes 1448 | tf_op jit(solution)/shard_map/ppermute | solution.py:20
  77.7 16.7 %all-to-all-start = ((bf16[16,16,542]{2,1,0:T(8,128)(2,1)}), bf16[16,16,542]{2,1,0:T(8,128)(2,1)S(1)}, u32[]{:S(2)}, u32[]{:S(2)}) async-start(bf16[16,16,542]{2,1,0:T(8,128)(2,1)} %stack.224), calls=%async_computation | async-start | bytes 655360 | tf_op jit(solution)/shard_map/all_to_all | solution.py:63
  94.5 55.9 %all-to-all-start.1 = ((bf16[16,2,8192]{2,1,0:T(2,128)(2,1)}), bf16[16,2,8192]{2,1,0:T(2,128)(2,1)S(1)}, u32[]{:S(2)}, u32[]{:S(2)}) async-start(bf16[16,2,8192]{2,1,0:T(2,128)(2,1)} %reshape.75), calls=%async_computation.1 | async-start | bytes 1048576 | tf_op jit(solution)/shard_map/all_to_all | solution.py:78
  156.1 25.1 %copy-start.1 = (bf16[16,512]{1,0:T(8,128)(2,1)S(1)}, bf16[16,512]{1,0:T(8,128)(2,1)}, u32[]{:S(2)}) copy-start(bf16[16,512]{1,0:T(8,128)(2,1)} %param.6) | copy-start | bytes 49156
  169.9 5.6 %collective-permute-start.2 = (bf16[16,15]{1,0:T(8,128)(2,1)S(1)}, bf16[16,15]{1,0:T(8,128)(2,1)S(1)}, u32[]{:S(2)}, u32[]{:S(2)}) collective-permute-start(bf16[16,15]{1,0:T(8,128)(2,1)S(1)} %get-tuple-element.34), channel_id=1, source_target_pairs={{0,16},{16,32},{32,48},{48,64},{64,80},{80,96},{96,112},{112,128},... | collective-permute-start | bytes 1448 | tf_op jit(solution)/shard_map/ppermute | solution.py:18
  171.8 5.0 %collective-permute-start.3 = (bf16[16,15]{1,0:T(8,128)(2,1)S(1)}, bf16[16,15]{1,0:T(8,128)(2,1)S(1)}, u32[]{:S(2)}, u32[]{:S(2)}) collective-permute-start(bf16[16,15]{1,0:T(8,128)(2,1)S(1)} %get-tuple-element.35), channel_id=1, source_target_pairs={{16,0},{32,16},{48,32},{64,48},{80,64},{96,80},{112,96},{128,112},... | collective-permute-start | bytes 1448 | tf_op jit(solution)/shard_map/ppermute | solution.py:20
  177.6 18.8 %all-to-all-start.2 = ((bf16[16,16,542]{2,1,0:T(8,128)(2,1)}), bf16[16,16,542]{2,1,0:T(8,128)(2,1)S(1)}, u32[]{:S(2)}, u32[]{:S(2)}) async-start(bf16[16,16,542]{2,1,0:T(8,128)(2,1)} %stack.256), calls=%async_computation.2 | async-start | bytes 655360 | tf_op jit(solution)/shard_map/all_to_all | solution.py:63
  196.4 4.3 %copy-start = (bf16[30,256,256]{2,1,0:T(8,128)(2,1)S(1)}, bf16[30,256,256]{2,1,0:T(8,128)(2,1)}, u32[]{:S(2)}) copy-start(bf16[30,256,256]{2,1,0:T(8,128)(2,1)} %param.8) | copy-start | bytes 11796484
  196.4 4.3 %copy-start.2 = (bf16[16,512]{1,0:T(8,128)(2,1)S(1)}, bf16[16,512]{1,0:T(8,128)(2,1)}, u32[]{:S(2)}) copy-start(bf16[16,512]{1,0:T(8,128)(2,1)} %param.7) | copy-start | bytes 49156
